TPU v7x, 128 devices: a whole 4x4x4 slice. The times are simulated.
128 devices in a mesh: bf: 8 (over y_lo, z), sk: 16 (over x, y_hi, core).
Axes of the slice: x: 4, y: 4 (y_hi: 2, y_lo: 2; y = y_hi * 2 + y_lo), z: 4, core: 2. Of those that a mesh axis runs over, the one named last changes fastest.
Arguments:
- kernel: bfloat16 [2, 16384, 32768], P(None, 'bf', 'sk'), may hold values from -1.1048543 to 1.1048543
- sketch: bfloat16 [3, 32768, 256], P(None, 'sk'), may hold values from -6 to 6
- projections: bfloat16 [2, 8, 2, 256, 128], P(None, 'bf'), may hold values from -0.375 to 0.375
- inverses: bfloat16 [2, 8, 2, 256, 256], P(None, 'bf'), may hold values from -0.375 to 0.375
- norm_gain: float32 [256], replicated, may hold values from 0.5 to 1.5
Outputs:
- factor_sketch: float32 [2, 3, 16384, 256], P(None, None, ('bf', 'sk'))
All inputs are finite; a program needn't handle non-finite values.
Results may differ from a plain program's by a relative error of at most 0.02.
Values may be sent and summed in bfloat16 or wider, within the bound.
A program may use at most 128 MiB of HBM per device.

v0:
```python
import jax
import jax.numpy as jnp
from jax import lax
from jax.sharding import Mesh
from jax.sharding import PartitionSpec as P

SK = ("sk_0", "sk_1", "sk_2")
BF_SK = ("bf", "sk_0", "sk_1", "sk_2")


epsilon = 1e-06


def split_up(shard, dim, peers):
    before, after = (shard.shape[:dim], shard.shape[dim + 1 :])
    return jnp.moveaxis(shard.reshape(*before, peers, -1, *after), dim, 0)


def sent_and_summed(shard, axis, dim):
    peers = lax.axis_size(axis)
    blocks = lax.all_to_all(split_up(shard, dim, peers), axis, 0, 0, tiled=True)
    return jnp.sum(blocks.astype(jnp.float32), axis=0)


def summed_rows(shard, axes, dim):
    far, near = axes
    own = sent_and_summed(split_up(shard, dim, lax.axis_size(far)), near, dim + 1)
    return jnp.sum(
        lax.all_to_all(own.astype(jnp.bfloat16), far, 0, 0, tiled=True).astype(jnp.float32), axis=0
    )


def swapped(value, axis, bit):
    mask = 2**bit
    pairs = [(source, source ^ mask) for source in range(lax.axis_size(axis))]
    return lax.ppermute(value, axis, pairs)


def complex_block(matrix):
    upper = jnp.concatenate([matrix[0], matrix[1]], axis=1)
    lower = jnp.concatenate([-matrix[1], matrix[0]], axis=1)
    return jnp.concatenate([upper, lower], axis=0)


def shards(kernel, sketch, projections, inverses, norm_gain):
    rank_cols = projections.shape[4]
    first_proj = projections[0, 0]
    both_parts = jnp.concatenate([first_proj[0], first_proj[1]], axis=1)
    sk_proj = jnp.einsum(
        "pcs,sk->pck", sketch, both_parts, preferred_element_type=jnp.float32
    ).astype(jnp.bfloat16)
    turned = jnp.concatenate([-sk_proj[:, :, rank_cols:], sk_proj[:, :, :rank_cols]], axis=2)
    partial_value = jnp.einsum(
        "rc,pck->prk", kernel[0], sk_proj, preferred_element_type=jnp.float32
    )
    partial_value = partial_value + jnp.einsum(
        "rc,pck->prk", kernel[1], turned, preferred_element_type=jnp.float32
    )
    summed = summed_rows(partial_value.astype(jnp.bfloat16), (("sk_0", "sk_1"), "sk_2"), 1)
    own_proj = summed.astype(jnp.bfloat16)
    top_bits = lax.axis_size("bf").bit_length() - 1
    current = summed
    for level_idx in range(projections.shape[0]):
        level_bit = top_bits - 1 - level_idx
        if level_idx > 0:
            rounded = current.astype(jnp.bfloat16)
            level_mat = complex_block(projections[level_idx, 0])
            own_proj = jnp.einsum(
                "prs,sk->prk", rounded, level_mat, preferred_element_type=jnp.float32
            ).astype(jnp.bfloat16)
        partner = swapped(own_proj, "bf", level_bit)
        solver = inverses[level_idx, 0]
        own_mat = complex_block(solver[:, :rank_cols])
        partner_mat = complex_block(solver[:, rank_cols:])
        current = jnp.einsum("prk,ks->prs", own_proj, own_mat, preferred_element_type=jnp.float32)
        current = current + jnp.einsum(
            "prk,ks->prs", partner, partner_mat, preferred_element_type=jnp.float32
        )
    sketch_cols = current.shape[2] // 2
    power = jnp.sum(current * current, axis=-1, keepdims=True) / sketch_cols
    scaled = current * lax.rsqrt(power + epsilon)
    return jnp.stack(
        [scaled[:, :, :sketch_cols] * norm_gain, scaled[:, :, sketch_cols:] * norm_gain]
    )


def solution(mesh):
    torus = Mesh(mesh.devices.reshape(mesh.shape["bf"], 4, 2, 2), ("bf", "sk_0", "sk_1", "sk_2"))
    in_specs = (
        P(None, "bf", SK),
        P(None, SK, None),
        P(None, "bf", None, None, None),
        P(None, "bf", None, None, None),
        P(),
    )
    out_specs = P(None, None, BF_SK, None)
    return jax.shard_map(
        shards, mesh=torus, in_specs=in_specs, out_specs=out_specs, check_vma=False
    )
```

profile of v0, /device:TPU:0, one launch (start us, length us, event | category | flops | bytes accessed | tf_op | source)
XLA Modules:
  0.0 107.4 jit_solution(4306408842934691482)
XLA Ops:
  0.0 0.0 copy-start
  0.0 1.8 %slice_bitcast_fusion.10 = (bf16[256,128]{1,0:T(8,128)(2,1)}, bf16[1,1,1,256,128]{4,3,2,1,0:T(8,128)(2,1)S(1)}, bf16[1,1,1,256,128]{4,3,2,1,0:T(8,128)(2,1)S(1)}, bf16[256,128]{1,0:T(8,128)(2,1)}) fusion(bf16[2,1,2,256,128]{4,3,2,1,0:T(8,128)(2,1)} %param.7), kind=kLoop, calls=%fused_computation.75 | loop fusion | bytes 524288 | tf_op jit(solution)/shard_map/squeeze | solution.py:40
  1.8 0.1 copy.28
  1.9 0.1 copy.29
  2.0 0.0 copy-done
  2.0 1.0 fusion.11
  3.0 0.2 slice_negate_fusion
  3.2 10.9 %fusion = f32[3,256,2048]{2,1,0:T(8,128)} fusion(bf16[2,2048,2048]{2,1,0:T(8,128)(2,1)} %param.5, bf16[3,2048,128]{1,2,0:T(8,128)(2,1)S(1)} %get-tuple-element.6, bf16[3,2048,128]{1,2,0:T(8,128)(2,1)S(1)} %get-tuple-element.5), kind=kOutput, calls=%fused_computation | convolution fusion | flops 6448742400 | bytes 17825792 | tf_op jit(solution)/shard_map/rc,pck->prk/dot_general | solution.py:56
  14.1 11.2 %add_convert_fusion = bf16[3,256,2048]{2,1,0:T(8,128)(2,1)S(1)} fusion(f32[3,256,2048]{2,1,0:T(8,128)} %fusion, bf16[3,2048,256]{1,2,0:T(8,128)(2,1)S(1)} %fusion.11, bf16[2,2048,2048]{2,1,0:T(8,128)(2,1)} %param.5), kind=kOutput, calls=%fused_computation.6 | convolution fusion | flops 6445596672 | bytes 20971520 | tf_op jit(solution)/shard_map/rc,pck->prk/dot_general | solution.py:53
  25.3 2.8 %copy.30 = bf16[96,8,8,256]{3,2,1,0:T(8,128)(2,1)} copy(bf16[96,8,8,256]{3,1,2,0:T(8,128)(2,1)S(1)} %bitcast.93) | data formatting | bytes 6291456
  28.0 4.9 %copy.18 = bf16[3,8,256,256]{3,2,0,1:T(8,128)(2,1)} copy(bf16[3,8,256,256]{2,1,3,0:T(8,128)(2,1)} %bitcast.91) | data formatting | bytes 6291456 | tf_op jit(solution)/shard_map/reshape | solution.py:16
  33.0 4.8 %copy.19 = bf16[2,8,3,128,256]{3,1,4,2,0:T(8,128)(2,1)} copy(bf16[2,8,3,128,256]{4,3,0,2,1:T(8,128)(2,1)} %bitcast.92) | data formatting | bytes 6291456 | tf_op jit(solution)/shard_map/transpose | solution.py:16
  37.8 10.3 %all_to_all.10 = bf16[2,8,3,128,256]{3,1,4,2,0:T(8,128)(2,1)} all-to-all(bf16[2,8,3,128,256]{3,1,4,2,0:T(8,128)(2,1)} %copy.19), channel_id=1, replica_groups=mesh['bf'=8,'sk_0'=4,'sk_1'=2,'sk_2'=2] {'sk_2'}, dimensions={0} | all-to-all | bytes 6291456 | tf_op jit(solution)/shard_map/all_to_all | solution.py:21
  48.2 4.0 %reduce_sum.33 = bf16[8,3,128,256]{2,0,3,1:T(8,128)(2,1)} reduce(bf16[2,8,3,128,256]{3,1,4,2,0:T(8,128)(2,1)} %all_to_all.10, bf16[]{:T(256)} %constant.6.clone.1), dimensions={0}, to_apply=%region_0.0 | reduce | flops 786432 | bytes 4718594 | tf_op jit(solution)/shard_map/reduce_sum | solution.py:22
  52.2 2.9 %copy.21 = bf16[8,3,128,256]{2,3,1,0:T(8,128)(2,1)} copy(bf16[8,3,128,256]{2,0,3,1:T(8,128)(2,1)} %reduce_sum.33) | data formatting | bytes 3145728 | tf_op jit(solution)/shard_map/reduce_sum | solution.py:22
  55.1 7.0 %all-to-all-start.1 = ((bf16[8,3,128,256]{2,3,1,0:T(8,128)(2,1)}), bf16[8,3,128,256]{2,3,1,0:T(8,128)(2,1)}, u32[]{:S(2)}, u32[]{:S(2)}) async-start(bf16[8,3,128,256]{2,3,1,0:T(8,128)(2,1)} %copy.21), calls=%async_computation.1 | async-start | bytes 3145728 | tf_op jit(solution)/shard_map/all_to_all | solution.py:29
  62.1 1.5 %fusion.64 = bf16[256,128]{1,0:T(8,128)(2,1)} fusion(bf16[2,1,2,256,128]{4,3,2,1,0:T(8,128)(2,1)} %param.7), kind=kLoop, calls=%fused_computation.84 | loop fusion | flops 32768 | bytes 131072 | tf_op jit(solution)/shard_map/neg | solution.py:41
  63.6 1.1 slice_bitcast_fusion
  64.7 0.6 fusion.66
  65.3 0.6 fusion.68
  65.9 0.7 slice_bitcast_fusion.6
  66.6 0.7 slice_bitcast_fusion.2
  67.3 19.1 %all-to-all-done.1 = bf16[8,3,128,256]{2,3,1,0:T(8,128)(2,1)} async-done(((bf16[8,3,128,256]{2,3,1,0:T(8,128)(2,1)}), bf16[8,3,128,256]{2,3,1,0:T(8,128)(2,1)}, u32[]{:S(2)}, u32[]{:S(2)}) %all-to-all-start.1) | async-done | bytes 1572896 | tf_op jit(solution)/shard_map/all_to_all | solution.py:29
  86.4 1.7 %reduce_sum.34 = bf16[3,128,256]{1,2,0:T(8,128)(2,1)S(1)} reduce(bf16[8,3,128,256]{2,3,1,0:T(8,128)(2,1)} %all-to-all-done.1, bf16[]{:T(256)} %constant.6.clone.1), dimensions={0}, to_apply=%region_1.0 | reduce | flops 688128 | bytes 1769474 | tf_op jit(solution)/shard_map/reduce_sum | solution.py:28
  88.1 0.8 copy.24
  88.9 0.7 collective-permute-start
  89.6 2.1 %fusion.17 = f32[3,128,512]{2,1,0:T(8,128)} fusion(bf16[3,128,256]{1,2,0:T(8,128)(2,1)S(1)} %reduce_sum.34, bf16[128,256]{1,0:T(8,128)(2,1)} %get-tuple-element.24, bf16[128,256]{1,0:T(8,128)(2,1)S(1)} %get-tuple-element.26, bf16[128,256]{1,0:T(8,128)(2,1)} %get-tuple-element.23), kind=kOutput, calls=%fused_computation.26 | convolution fusion | flops 101711872 | bytes 1179648 | tf_op jit(solution)/shard_map/prk,ks->prs/dot_general | solution.py:75
  91.7 0.0 copy-start.1
  91.7 3.3 %collective-permute-done = bf16[3,128,256]{2,1,0:T(8,128)(2,1)S(1)} collective-permute-done((bf16[3,128,256]{2,1,0:T(8,128)(2,1)}, bf16[3,128,256]{2,1,0:T(8,128)(2,1)S(1)}, u32[]{:S(2)}, u32[]{:S(2)}) %collective-permute-start) | collective-permute-done | bytes 196640 | tf_op jit(solution)/shard_map/ppermute | solution.py:36
  95.0 0.0 copy-start.3
  95.0 0.7 copy-done.3
  95.7 0.0 copy-start.2
  95.7 2.5 %fusion.14 = bf16[3,128,256]{2,1,0:T(8,128)(2,1)} fusion(f32[3,128,512]{2,1,0:T(8,128)} %fusion.17, bf16[3,128,256]{2,1,0:T(8,128)(2,1)} %copy-done.3, bf16[128,256]{1,0:T(8,128)(2,1)} %get-tuple-element.22, bf16[128,256]{1,0:T(8,128)(2,1)} %get-tuple-element.25, bf16[128,256]{1,0:T(8,128)(2,1)} %get-tuple-element.21, ...), kind=kOutput, calls=%fused_computation.17 | convolution fusion | flops 203915264 | bytes 1572864 | tf_op jit(solution)/shard_map/prs,sk->prk/dot_general | solution.py:68
  98.2 3.9 %collective-permute-start.1 = (bf16[3,128,256]{2,1,0:T(8,128)(2,1)}, bf16[3,128,256]{2,1,0:T(8,128)(2,1)S(1)}, u32[]{:S(2)}, u32[]{:S(2)}) collective-permute-start(bf16[3,128,256]{2,1,0:T(8,128)(2,1)} %fusion.14), channel_id=1, source_target_pairs={{0,32},{16,48},{32,0},{48,16},{64,96},{80,112},{96,64},{112,80},{1... | collective-permute-start | bytes 589832 | tf_op jit(solution)/shard_map/ppermute | solution.py:36
  102.1 1.3 %fusion.42 = f32[3,128,512]{2,1,0:T(8,128)S(1)} fusion(bf16[3,128,256]{2,1,0:T(8,128)(2,1)} %fusion.14, bf16[128,256]{1,0:T(8,128)(2,1)} %get-tuple-element.14, bf16[128,256]{1,0:T(8,128)(2,1)} %get-tuple-element.16, bf16[128,256]{1,0:T(8,128)(2,1)} %get-tuple-element.13), kind=kOutput, calls=%fused_computation.48 | convolution fusion | flops 101711872 | bytes 1179648 | tf_op jit(solution)/shard_map/prk,ks->prs/dot_general | solution.py:75
  103.4 2.6 %collective-permute-done.1 = bf16[3,128,256]{2,1,0:T(8,128)(2,1)S(1)} collective-permute-done((bf16[3,128,256]{2,1,0:T(8,128)(2,1)}, bf16[3,128,256]{2,1,0:T(8,128)(2,1)S(1)}, u32[]{:S(2)}, u32[]{:S(2)}) %collective-permute-start.1) | collective-permute-done | bytes 196640 | tf_op jit(solution)/shard_map/ppermute | solution.py:36
  105.9 0.0 copy-done.1
  105.9 0.3 multiply_reduce_fusion
  106.3 0.1 broadcast_multiply_fusion
  106.4 0.0 copy-done.2
  106.4 0.1 fusion.16
  106.5 0.9 pad_maximum_fusion
  (1 shorter events, 0.0 us)
Async XLA Ops:
  0.0 2.0 %copy-start = (bf16[3,2048,256]{2,1,0:T(8,128)(2,1)S(1)}, bf16[3,2048,256]{2,1,0:T(8,128)(2,1)}, u32[]{:S(2)}) copy-start(bf16[3,2048,256]{2,1,0:T(8,128)(2,1)} %param.6) | copy-start | bytes 9437188
  55.1 31.3 %all-to-all-start.1 = ((bf16[8,3,128,256]{2,3,1,0:T(8,128)(2,1)}), bf16[8,3,128,256]{2,3,1,0:T(8,128)(2,1)}, u32[]{:S(2)}, u32[]{:S(2)}) async-start(bf16[8,3,128,256]{2,3,1,0:T(8,128)(2,1)} %copy.21), calls=%async_computation.1 | async-start | bytes 3145728 | tf_op jit(solution)/shard_map/all_to_all | solution.py:29
  88.9 6.1 %collective-permute-start = (bf16[3,128,256]{2,1,0:T(8,128)(2,1)}, bf16[3,128,256]{2,1,0:T(8,128)(2,1)S(1)}, u32[]{:S(2)}, u32[]{:S(2)}) collective-permute-start(bf16[3,128,256]{2,1,0:T(8,128)(2,1)} %copy.24), channel_id=1, source_target_pairs={{0,64},{16,80},{32,96},{48,112},{64,0},{80,16},{96,32},{112,48},{1... | collective-permute-start | bytes 589832 | tf_op jit(solution)/shard_map/ppermute | solution.py:36
  91.7 14.2 %copy-start.1 = (bf16[128,256]{1,0:T(8,128)(2,1)S(1)}, bf16[128,256]{1,0:T(8,128)(2,1)}, u32[]{:S(2)}) copy-start(bf16[128,256]{1,0:T(8,128)(2,1)} %get-tuple-element.12) | copy-start | bytes 196612
  95.0 0.7 copy-start.3
  95.7 10.7 %copy-start.2 = (f32[256]{0:T(256)S(1)}, f32[256]{0:T(256)}, u32[]{:S(2)}) copy-start(f32[256]{0:T(256)} %param.9) | copy-start | bytes 3076
  98.2 7.7 %collective-permute-start.1 = (bf16[3,128,256]{2,1,0:T(8,128)(2,1)}, bf16[3,128,256]{2,1,0:T(8,128)(2,1)S(1)}, u32[]{:S(2)}, u32[]{:S(2)}) collective-permute-start(bf16[3,128,256]{2,1,0:T(8,128)(2,1)} %fusion.14), channel_id=1, source_target_pairs={{0,32},{16,48},{32,0},{48,16},{64,96},{80,112},{96,64},{112,80},{1... | collective-permute-start | bytes 589832 | tf_op jit(solution)/shard_map/ppermute | solution.py:36
where the time goes:
time: 108 us; the launch traced here: 107 us
  matrix products  29.2 us (27%)
  waiting for transfers between devices  25 us (23%)
  local copies, waits for them, and re-layouts  21.4 us (20%)
  starting transfers between devices  11.6 us (11%)
  blocking collectives  10.3 us (10%)
  other arithmetic  9.76 us (9%)
    all_to_all x1, waiting for transfers between devices, summed_rows(): lax.all_to_all(own.astype(jnp.bfloat16), far, 0, 0, tiled=True)  19.1 us
    dot_general x1, matrix products, shards(): jnp.einsum('rc,pck->prk', kernel[0], sk_proj, preferred_element_type=jnp....  11.2 us
    dot_general x1, matrix products, shards(): jnp.einsum('rc,pck->prk', kernel[1], turned, preferred_element_type=jnp.f...  10.9 us
    all_to_all x1, blocking collectives, sent_and_summed(): blocks = lax.all_to_all(split_up(shard, dim, peers), axis, 0, 0, tiled=True)  10.3 us
    all_to_all x1, starting transfers between devices, summed_rows(): lax.all_to_all(own.astype(jnp.bfloat16), far, 0, 0, tiled=True)  7.04 us
    ppermute x2, waiting for transfers between devices, swapped(): return lax.ppermute(value, axis, pairs)  5.9 us
    reshape x1, local copies, waits for them, and re-layouts, split_up(): return jnp.moveaxis(shard.reshape(*before, peers, -1, *after), dim, 0)  4.94 us
    transpose x1, local copies, waits for them, and re-layouts, split_up(): return jnp.moveaxis(shard.reshape(*before, peers, -1, *after), dim, 0)  4.85 us
  transfers between devices with their start and end apart: 3, of which 3 were waited for; matrix products, arithmetic and copies ran while one was open for 8% of the time, Pallas kernels for 0%

commit v1 on v0

v1 whole, which is shorter than its diff:
```python
import functools

import jax
import jax.numpy as jnp
from jax import lax
from jax.experimental import pallas as pl
from jax.experimental.pallas import tpu as pltpu
from jax.sharding import Mesh
from jax.sharding import PartitionSpec as P

AXES = ("yl", "z", "x", "yh", "c")
MESH = pl.DeviceIdType.MESH
F32 = jnp.float32
BF16 = jnp.bfloat16
EPSILON = 1e-06


def complex_block(real, imag):
    upper = jnp.concatenate([real, imag], axis=1)
    lower = jnp.concatenate([-imag, real], axis=1)
    return jnp.concatenate([upper, lower], axis=0)


def dot(a, b):
    return jnp.dot(a, b, preferred_element_type=F32)


def kernel(
    k_hbm, s_hbm, proj_hbm, inv_hbm, gain_hbm, o_hbm,
    kv, sv, sp, projv, invv, gainv, mats, mats_far, last_mats,
    own, c_send, c_recv, x_send, x_recv,
    half, y1_send, y1_recv, held, y2_send, y2_recv, own1, z_recv, outv,
    k_sem, s_sem, w_sem, o_sem, m_sems, c_sems, x_sems, y1_sems, y2_sems, z_sems,
):
    yl, z, x, yh, c = (lax.axis_index(a) for a in AXES)
    passes = 3
    far_x = lax.rem(x + 2, 4)
    right = lax.rem(x + 1, 4)
    left = lax.rem(x + 3, 4)
    core_peer = (yl, z, x, yh, 1 - c)
    right_peer = (yl, z, right, yh, c)
    left_peer = (yl, z, left, yh, c)
    y1_peer = (1 - yl, z, x, 1 - yh, c)
    y2_peer = (1 - yl, z, x, yh, c)
    z_peer = (yl, lax.rem(z + 2, 4), x, yh, c)

    units = (
        ((far_x, 0), (far_x, 1)),
        ((right, 1), (left, 0)),
        ((right, 0), (left, 1)),
        ((x, 0), (x, 1)),
    )

    def k_copies(j):
        copies = []
        for part in range(2):
            for core, core_idx in enumerate((1 - c, c)):
                for u in range(2):
                    dest_x, dest_yh = units[j][u]
                    row = pl.multiple_of(((dest_x * 2 + dest_yh) * 2 + core_idx) * 128, 128)
                    copies.append(
                        pltpu.make_async_copy(
                            k_hbm.at[part, pl.ds(row, 128), :],
                            kv.at[j, part, pl.ds((core * 2 + u) * 128, 128), :],
                            k_sem.at[j, part, core * 2 + u],
                        )
                    )
        return copies

    def s_copy(p):
        return pltpu.make_async_copy(s_hbm.at[p], sv.at[p], s_sem.at[p])

    w_copies = (
        pltpu.make_async_copy(proj_hbm, projv, w_sem.at[0]),
        pltpu.make_async_copy(inv_hbm, invv, w_sem.at[1]),
        pltpu.make_async_copy(gain_hbm, gainv, w_sem.at[2]),
    )

    def remote(src, dst, sems, index, peer):
        return pltpu.make_async_remote_copy(
            src_ref=src,
            dst_ref=dst,
            send_sem=sems.at[(0,) + index],
            recv_sem=sems.at[(1,) + index],
            device_id=peer,
            device_id_type=MESH,
        )

    def m_copy():
        return remote(mats, mats_far, m_sems, (), y2_peer)

    def c_copy(p, j):
        return remote(c_send.at[p, j], c_recv.at[p, j], c_sems, (p, j), core_peer)

    def x_copy(p, j, u):
        peer = (right_peer, left_peer)[u]
        return remote(x_send.at[p, j, u], x_recv.at[p, j, u], x_sems, (p, j, u), peer)

    def y1_copy(p):
        return remote(y1_send.at[p], y1_recv.at[p], y1_sems, (p,), y1_peer)

    def y2_copy(p):
        return remote(y2_send.at[p], y2_recv.at[p], y2_sems, (p,), y2_peer)

    def z_copy(p):
        return remote(own1.at[p], z_recv.at[p], z_sems, (p,), z_peer)

    def o_copy(p):
        return pltpu.make_async_copy(outv.at[p], o_hbm.at[:, p], o_sem.at[p])

    w_copies[0].start()
    s_copy(0).start()
    for copy in k_copies(0):
        copy.start()
    w_copies[1].start()
    w_copies[2].start()
    for copy in k_copies(1):
        copy.start()
    s_copy(1).start()
    for copy in k_copies(2):
        copy.start()
    for copy in k_copies(3):
        copy.start()
    s_copy(2).start()

    barrier = pltpu.get_barrier_semaphore()
    for peer in (core_peer, right_peer, left_peer, y1_peer, y2_peer, z_peer):
        pl.semaphore_signal(barrier, inc=1, device_id=peer, device_id_type=MESH)

    def project(p):
        s_copy(p).wait()
        both = jnp.concatenate([projv[0, 0, 0], projv[0, 0, 1]], axis=1)
        for step in range(4):
            rows = pl.ds(step * 512, 512)
            part = dot(sv[p, rows, :], both).astype(BF16)
            sp[p, 0, rows, :] = part
            sp[p, 1, rows, :] = jnp.concatenate([-part[:, 128:], part[:, :128]], axis=1)

    w_copies[0].wait()
    project(0)
    w_copies[1].wait()
    w_copies[2].wait()
    level = complex_block(projv[1, 0, 0], projv[1, 0, 1])
    for i in range(2):
        rows = pl.ds(i * 128, 128)
        first = complex_block(invv[0, 0, 0, rows, :], invv[0, 0, 1, rows, :])
        mats[i] = dot(first, level).astype(BF16)
        last_mats[i] = complex_block(invv[1, 0, 0, rows, :], invv[1, 0, 1, rows, :])
    pl.semaphore_wait(barrier, 6)
    m_copy().start()

    def post(p, j):
        copy = c_copy(p, j)
        copy.wait_send()
        copy.wait_recv()
        for u in range(2):
            rows = pl.ds(u * 128, 128)
            unit = own[j, rows, :] + c_recv[p, j, rows, :].astype(F32)
            if j == 2:
                x_copy(p, 0, u).wait_recv()
                unit = unit + x_recv[p, 0, u].astype(F32)
            x_send[p, j, u] = unit.astype(BF16)
            x_copy(p, j, u).start()

    def finish_x(p):
        copy = c_copy(p, 3)
        copy.wait_send()
        copy.wait_recv()
        for j in (1, 2):
            for u in range(2):
                x_copy(p, j, u).wait_recv()
        for u in range(2):
            rows = pl.ds(u * 128, 128)
            half[u] = (
                own[3, rows, :]
                + c_recv[p, 3, rows, :].astype(F32)
                + x_recv[p, 2 - u, 0].astype(F32)
                + x_recv[p, 1 + u, 1].astype(F32)
            ).astype(BF16)
        y1_send[p] = half[1 - yh]
        y1_copy(p).start()
        held[p, 0] = half[yh].astype(F32)

    def level_products(p):
        y1_copy(p).wait_recv()
        mine = held[p, 0].astype(BF16)
        other = y1_recv[p]
        y2_send[p] = (dot(mine, mats_far[1]) + dot(other, mats_far[0])).astype(BF16)
        y2_copy(p).start()
        held[p, 1] = dot(mine, mats[0]) + dot(other, mats[1])

    def level_own(p):
        y2_copy(p).wait_recv()
        own1[p] = (held[p, 1] + y2_recv[p].astype(F32)).astype(BF16)
        z_copy(p).start()

    def finish(p):
        z_copy(p).wait_recv()
        current = dot(own1[p], last_mats[0]) + dot(z_recv[p], last_mats[1])
        power = jnp.sum(current * current, axis=-1, keepdims=True) / 256
        scaled = current * lax.rsqrt(power + EPSILON)
        gain = gainv[...]
        outv[p, 0] = scaled[:, :256] * gain
        outv[p, 1] = scaled[:, 256:] * gain
        o_copy(p).start()

    def slab(g, _):
        p = g // 4
        j = lax.rem(g, 4)

        for first in range(4):

            @pl.when(g == first)
            def _():
                for copy in k_copies(first):
                    copy.wait()

        acc = dot(kv[j, 0], sp[p, 0]) + dot(kv[j, 1], sp[p, 1])
        c_send[p, j] = acc[:256].astype(BF16)
        c_copy(p, j).start()
        own[j] = acc[256:]

        for ahead in (1, 2):

            @pl.when(g == 4 * ahead - 4)
            def _():
                project(ahead)

        @pl.when(j == 1)
        def _():
            post(p, 0)

        @pl.when(j == 2)
        def _():
            post(p, 1)

        @pl.when(j == 3)
        def _():
            post(p, 2)

        @pl.when((j == 1) & (p >= 1))
        def _():
            finish_x(p - 1)

        @pl.when((j == 1) & (p >= 2))
        def _():
            level_own(p - 2)

        @pl.when((j == 3) & (p == 1))
        def _():
            m_copy().wait_recv()

        @pl.when((j == 3) & (p >= 1))
        def _():
            level_products(p - 1)

        return 0

    lax.fori_loop(0, 4 * passes, slab, 0)
    finish(0)
    finish_x(2)
    level_own(1)
    level_products(2)
    finish(1)
    level_own(2)
    finish(2)
    m_copy().wait_send()
    for p in range(passes):
        for u in range(2):
            for j in range(3):
                x_copy(p, j, u).wait_send()
        y1_copy(p).wait_send()
        y2_copy(p).wait_send()
        z_copy(p).wait_send()
        o_copy(p).wait()


def shards(kernel_shard, sketch, projections, inverses, norm_gain):
    dma = pltpu.SemaphoreType.DMA
    return pl.pallas_call(
        kernel,
        out_shape=jax.ShapeDtypeStruct((2, 3, 128, 256), F32),
        in_specs=[pl.BlockSpec(memory_space=pl.ANY)] * 5,
        out_specs=pl.BlockSpec(memory_space=pl.ANY),
        scratch_shapes=[
            pltpu.VMEM((4, 2, 512, 2048), BF16),
            pltpu.VMEM((3, 2048, 256), BF16),
            pltpu.VMEM((3, 2, 2048, 256), BF16),
            pltpu.VMEM((2, 1, 2, 256, 128), BF16),
            pltpu.VMEM((2, 1, 2, 256, 256), BF16),
            pltpu.VMEM((1, 256), F32),
            pltpu.VMEM((2, 256, 256), BF16),
            pltpu.VMEM((2, 256, 256), BF16),
            pltpu.VMEM((2, 256, 512), BF16),
            pltpu.VMEM((4, 256, 256), F32),
            pltpu.VMEM((3, 4, 256, 256), BF16),
            pltpu.VMEM((3, 4, 256, 256), BF16),
            pltpu.VMEM((3, 3, 2, 128, 256), BF16),
            pltpu.VMEM((3, 3, 2, 128, 256), BF16),
            pltpu.VMEM((2, 128, 256), BF16),
            pltpu.VMEM((3, 128, 256), BF16),
            pltpu.VMEM((3, 128, 256), BF16),
            pltpu.VMEM((3, 2, 128, 256), F32),
            pltpu.VMEM((3, 128, 256), BF16),
            pltpu.VMEM((3, 128, 256), BF16),
            pltpu.VMEM((3, 128, 256), BF16),
            pltpu.VMEM((3, 128, 256), BF16),
            pltpu.VMEM((3, 2, 128, 256), F32),
            dma((4, 2, 4)),
            dma((3,)),
            dma((3,)),
            dma((3,)),
            dma((2,)),
            dma((2, 3, 4)),
            dma((2, 3, 3, 2)),
            dma((2, 3)),
            dma((2, 3)),
            dma((2, 3)),
        ],
        compiler_params=pltpu.CompilerParams(
            collective_id=0, has_side_effects=True, vmem_limit_bytes=56 << 20
        ),
        name="butterfly",
    )(kernel_shard, sketch, projections, inverses, norm_gain.reshape(1, 256))


def solution(mesh):
    torus = Mesh(mesh.devices.reshape(2, 4, 4, 2, 2), AXES)
    in_specs = (
        P(None, ("yl", "z"), ("x", "yh", "c")),
        P(None, ("x", "yh", "c"), None),
        P(None, ("yl", "z"), None, None, None),
        P(None, ("yl", "z"), None, None, None),
        P(),
    )
    return jax.shard_map(
        shards, mesh=torus, in_specs=in_specs, out_specs=P(None, None, AXES, None), check_vma=False
    )
```

time: 108 us -> 51.2 us (0.47)
  Pallas kernels: 0 us -> 48.9 us
  matrix products: 29.2 us -> 0 us
  waiting for transfers between devices: 25 us -> 0 us
  local copies, waits for them, and re-layouts: 21.4 us -> 2.1 us
  starting transfers between devices: 11.6 us -> 0 us
  blocking collectives: 10.3 us -> 0 us
  other arithmetic: 9.76 us -> 0 us
    pallas_call x0 -> x1, Pallas kernels: none -> 48.9 us  [shards(): pl.pallas_call(kernel, out_shape=jax.ShapeDtypeStruct((2, 3, 128, 256), F...]
    dot_general x7 -> x0, matrix products: 29.2 us -> none  [the longest x1 11.2 us: shards(): jnp.einsum('rc,pck->prk', kernel[0], sk_proj, preferred_element_type=jnp....]
    all_to_all x1 -> x0, waiting for transfers between devices: 19.1 us -> none  [summed_rows(): lax.all_to_all(own.astype(jnp.bfloat16), far, 0, 0, tiled=True)]
    all_to_all x1 -> x0, blocking collectives: 10.3 us -> none  [sent_and_summed(): blocks = lax.all_to_all(split_up(shard, dim, peers), axis, 0, 0, tiled=True)]
    all_to_all x1 -> x0, starting transfers between devices: 7.04 us -> none  [summed_rows(): lax.all_to_all(own.astype(jnp.bfloat16), far, 0, 0, tiled=True)]
    ppermute x2 -> x0, waiting for transfers between devices: 5.9 us -> none  [swapped(): return lax.ppermute(value, axis, pairs)]
    reduce_sum x2 -> x0, other arithmetic: 5.68 us -> none  [the longest x1 4.01 us: sent_and_summed(): return jnp.sum(blocks.astype(jnp.float32), axis=0)]
    reshape x1 -> x0, local copies, waits for them, and re-layouts: 4.94 us -> none  [split_up(): return jnp.moveaxis(shard.reshape(*before, peers, -1, *after), dim, 0)]
  transfers between devices with their start and end apart: 3 -> 0, of which waited for: 3 -> 0; matrix products, arithmetic and copies ran while one was open for 8% -> 0% of each run, Pallas kernels for 0% -> 0%
where the time goes in v1:
time: 51.2 us; the launch traced here: 51 us
  Pallas kernels  48.9 us (96%)
  local copies, waits for them, and re-layouts  2.1 us (4%)
    pallas_call x1, Pallas kernels, shards(): pl.pallas_call(kernel, out_shape=jax.ShapeDtypeStruct((2, 3, 128, 256), F...  48.9 us
    unnamed x1, local copies, waits for them, and re-layouts  2.1 us

profile of v1, /device:TPU:0, one launch (start us, length us, event | category | flops | bytes accessed | tf_op | source)
XLA Modules:
  0.0 51.0 jit_solution(1538719588241153672)
XLA Ops:
  0.0 48.9 %butterfly.1 = f32[2,3,128,256]{3,2,1,0:T(8,128)} custom-call(bf16[2,2048,2048]{2,1,0:T(8,128)(2,1)} %k_hbm.1, bf16[3,2048,256]{2,1,0:T(8,128)(2,1)} %s_hbm.1, bf16[2,1,2,256,128]{4,3,2,1,0:T(8,128)(2,1)} %proj_hbm.1, bf16[2,1,2,256,256]{4,3,2,1,0:T(8,128)(2,1)} %inv_hbm.1, f32[1,256]{1,0:T(1,128)} %bitcast.1), custom_call_target="tpu_custom_call" | custom-call | tf_op jit(solution)/shard_map/butterfly/pallas_call | solution.py:280
  48.9 2.1 %copy.7 = f32[2,3,128,256]{3,2,1,0:T(8,128)} copy(f32[2,3,128,256]{3,2,1,0:T(8,128)} %butterfly.1) | data formatting | bytes 1572864

commit v2 on v1

v2 whole, which is shorter than its diff:
```python
import jax
import jax.numpy as jnp
from jax import lax
from jax.experimental import pallas as pl
from jax.experimental.pallas import tpu as pltpu
from jax.sharding import Mesh
from jax.sharding import PartitionSpec as P

AXES = ("yl", "z", "x", "yh", "c")
MESH = pl.DeviceIdType.MESH
F32 = jnp.float32
BF16 = jnp.bfloat16
EPSILON = 1e-06
PASSES = 3
LAST = PASSES - 1


def complex_block(real, imag):
    upper = jnp.concatenate([real, imag], axis=1)
    lower = jnp.concatenate([-imag, real], axis=1)
    return jnp.concatenate([upper, lower], axis=0)


def dot(a, b):
    return jnp.dot(a, b, preferred_element_type=F32)


def span(p, h):
    return pl.ds(h * 64, 64) if p == LAST else pl.ds(0, 128)


def reduce_kernel(
    k_hbm, s_hbm, proj_hbm, inv_hbm, own1_out, far1_out, mats_out,
    kv, sv, pair, single, projv, invv, mats, mats_far,
    own, c_send, c_recv, x_send, x_recv,
    mine, y1_send, y1_recv, held, y2_send, y2_recv, own1, z_recv,
    k_sem, s_sem, w_sem, m_sems, c_sems, x_sems, y1_sems, y2_sems, z_sems,
):
    yl, z, x, yh, c = (lax.axis_index(a) for a in AXES)
    far_x = lax.rem(x + 2, 4)
    right = lax.rem(x + 1, 4)
    left = lax.rem(x + 3, 4)
    core_peer = (yl, z, x, yh, 1 - c)
    right_peer = (yl, z, right, yh, c)
    left_peer = (yl, z, left, yh, c)
    y1_peer = (1 - yl, z, x, 1 - yh, c)
    y2_peer = (1 - yl, z, x, yh, c)
    z_peer = (yl, lax.rem(z + 2, 4), x, yh, c)

    units = (
        ((far_x, 0), (far_x, 1)),
        ((right, 1), (left, 0)),
        ((right, 0), (left, 1)),
        ((x, 0), (x, 1)),
    )

    def start_slab(j):
        def start_part(part, _):
            for core, core_idx in enumerate((1 - c, c)):
                for u in range(2):
                    dest_x, dest_yh = units[j][u]
                    row = pl.multiple_of(((dest_x * 2 + dest_yh) * 2 + core_idx) * 128, 128)
                    pltpu.make_async_copy(
                        k_hbm.at[part, pl.ds(row, 128), :],
                        kv.at[j, part, pl.ds((core * 2 + u) * 128, 128), :],
                        k_sem.at[j],
                    ).start()
            return 0

        lax.fori_loop(0, 2, start_part, 0)

    def wait_slab(j):
        pltpu.make_async_copy(k_hbm.at[:, pl.ds(0, 512), :], kv.at[j], k_sem.at[j]).wait()

    def s_copy(p):
        return pltpu.make_async_copy(s_hbm.at[p], sv.at[p], s_sem.at[p])

    proj_copy = pltpu.make_async_copy(proj_hbm, projv, w_sem.at[0])
    inv_copy = pltpu.make_async_copy(inv_hbm, invv, w_sem.at[1])

    def remote(src, dst, sems, index, peer):
        return pltpu.make_async_remote_copy(
            src_ref=src,
            dst_ref=dst,
            send_sem=sems.at[(0,) + index],
            recv_sem=sems.at[(1,) + index],
            device_id=peer,
            device_id_type=MESH,
        )

    def m_copy():
        return remote(mats, mats_far, m_sems, (), y2_peer)

    def c_copy(p, j):
        return remote(c_send.at[p, j], c_recv.at[p, j], c_sems, (p, j), core_peer)

    def x_copy(p, j, u, h=0):
        peer = (right_peer, left_peer)[u]
        rows = span(p, h) if j == 2 else pl.ds(0, 128)
        at = (p, j, u, rows)
        return remote(x_send.at[at], x_recv.at[at], x_sems, (p, j + h, u), peer)

    def y1_copy(p, h):
        at = (p, span(p, h))
        return remote(y1_send.at[at], y1_recv.at[at], y1_sems, (p + h,), y1_peer)

    def y2_copy(p, h):
        at = (p, span(p, h))
        return remote(y2_send.at[at], y2_recv.at[at], y2_sems, (p + h,), y2_peer)

    def z_copy(p, h):
        at = (p, span(p, h))
        return remote(own1.at[at], z_recv.at[at], z_sems, (p + h,), z_peer)

    proj_copy.start()
    s_copy(0).start()
    s_copy(1).start()
    start_slab(0)
    inv_copy.start()
    start_slab(1)
    start_slab(2)
    start_slab(3)
    s_copy(2).start()

    barrier = pltpu.get_barrier_semaphore()
    for peer in (core_peer, right_peer, left_peer, y1_peer, y2_peer, z_peer):
        pl.semaphore_signal(barrier, inc=1, device_id=peer, device_id_type=MESH)

    proj_copy.wait()
    s_copy(0).wait()
    s_copy(1).wait()
    both = jnp.concatenate([projv[0, 0, 0], projv[0, 0, 1]], axis=1)
    for step in range(4):
        rows = pl.ds(step * 512, 512)
        first = dot(sv[0, rows, :], both).astype(BF16)
        second = dot(sv[1, rows, :], both).astype(BF16)
        real = jnp.concatenate([first[:, :128], second[:, :128]], axis=1)
        imag = jnp.concatenate([first[:, 128:], second[:, 128:]], axis=1)
        pair[0, rows, :] = real
        pair[1, rows, :] = imag
        pair[2, rows, :] = real + imag

    inv_copy.wait()
    level = complex_block(projv[1, 0, 0], projv[1, 0, 1])
    for i in range(2):
        rows = pl.ds(i * 128, 128)
        first = complex_block(invv[0, 0, 0, rows, :], invv[0, 0, 1, rows, :])
        mats[i] = dot(first, level).astype(BF16)
        mats_out[i] = complex_block(invv[1, 0, 0, rows, :], invv[1, 0, 1, rows, :])

    def project_last():
        s_copy(LAST).wait()
        both = jnp.concatenate([projv[0, 0, 0], projv[0, 0, 1]], axis=1)
        for step in range(4):
            rows = pl.ds(step * 512, 512)
            part = dot(sv[LAST, rows, :], both).astype(BF16)
            single[0, rows, :] = part
            single[1, rows, :] = jnp.concatenate([-part[:, 128:], part[:, :128]], axis=1)

    def post(p, j):
        copy = c_copy(p, j)
        copy.wait_send()
        copy.wait_recv()
        if j == 2:
            for u in range(2):
                x_copy(p, 0, u).wait_recv()
        for h in range(2 if p == LAST and j == 2 else 1):
            for u in range(2):
                rows = span(p, h) if j == 2 else pl.ds(0, 128)
                near = pl.ds(u * 128 + rows.start, rows.size)
                unit = own[p, j, near, :] + c_recv[p, j, near, :].astype(F32)
                if j == 2:
                    unit = unit + x_recv[p, 0, u, rows, :].astype(F32)
                x_send[p, j, u, rows, :] = unit.astype(BF16)
                x_copy(p, j, u, h).start()

    def finish_x(p, h):
        if h == 0:
            copy = c_copy(p, 3)
            copy.wait_send()
            copy.wait_recv()
            for u in range(2):
                x_copy(p, 1, u).wait_recv()
        for u in range(2):
            x_copy(p, 2, u, h).wait_recv()
        rows = span(p, h)

        def total(u):
            near = pl.ds(pl.multiple_of(u * 128 + rows.start, rows.size), rows.size)
            return (
                own[p, 3, near, :]
                + c_recv[p, 3, near, :].astype(F32)
                + x_recv[p, 2 - u, 0, rows, :].astype(F32)
                + x_recv[p, 1 + u, 1, rows, :].astype(F32)
            ).astype(BF16)

        y1_send[p, rows, :] = total(1 - yh)
        y1_copy(p, h).start()
        mine[p, rows, :] = total(yh)

    def level_products(p, h):
        y1_copy(p, h).wait_recv()
        rows = span(p, h)
        near = mine[p, rows, :]
        other = y1_recv[p, rows, :]
        y2_send[p, rows, :] = (dot(near, mats_far[1]) + dot(other, mats_far[0])).astype(BF16)
        y2_copy(p, h).start()
        held[p, rows, :] = dot(near, mats[0]) + dot(other, mats[1])

    def level_own(p, h):
        y2_copy(p, h).wait_recv()
        rows = span(p, h)
        value = (held[p, rows, :] + y2_recv[p, rows, :].astype(F32)).astype(BF16)
        own1[p, rows, :] = value
        z_copy(p, h).start()
        own1_out[p, rows, :] = value

    def finish(p, h):
        z_copy(p, h).wait_recv()
        rows = span(p, h)
        far1_out[p, rows, :] = z_recv[p, rows, :]

    def pair_slab(j, _):
        wait_slab(j)
        real_part = dot(kv[j, 0], pair[0])
        imag_part = dot(kv[j, 1], pair[1])
        cross = dot(kv[j, 0] + kv[j, 1], pair[2])
        real = real_part - imag_part
        imag = cross - real_part - imag_part

        @pl.when(j == 0)
        def _():
            pl.semaphore_wait(barrier, 6)

        for p in range(2):
            cols = slice(p * 128, (p + 1) * 128)
            acc = jnp.concatenate([real[:, cols], imag[:, cols]], axis=1)
            c_send[p, j] = acc[:256].astype(BF16)
            c_copy(p, j).start()
            own[p, j] = acc[256:]

        @pl.when(j == 0)
        def _():
            m_copy().start()

        for done in range(3):

            @pl.when(j == done + 1)
            def _():
                post(0, done)
                post(1, done)

        @pl.when(j == 2)
        def _():
            project_last()

        return 0

    def single_slab(j, _):
        acc = dot(kv[j, 0], single[0]) + dot(kv[j, 1], single[1])
        c_send[LAST, j] = acc[:256].astype(BF16)
        c_copy(LAST, j).start()
        own[LAST, j] = acc[256:]

        @pl.when(j == 1)
        def _():
            post(LAST, 0)

        @pl.when(j == 2)
        def _():
            post(LAST, 1)
            finish_x(0, 0)

        return 0

    lax.fori_loop(0, 4, pair_slab, 0)
    lax.fori_loop(0, 4, single_slab, 0)
    finish_x(1, 0)
    post(LAST, 2)
    m_copy().wait()
    level_products(0, 0)
    level_products(1, 0)
    finish_x(LAST, 0)
    finish_x(LAST, 1)
    level_own(0, 0)
    level_own(1, 0)
    level_products(LAST, 0)
    level_products(LAST, 1)
    level_own(LAST, 0)
    level_own(LAST, 1)
    finish(0, 0)
    finish(1, 0)
    finish(LAST, 0)
    finish(LAST, 1)
    for p in range(PASSES):
        for u in range(2):
            for j in range(3):
                x_copy(p, j, u).wait_send()
        y1_copy(p, 0).wait_send()
        y2_copy(p, 0).wait_send()
        z_copy(p, 0).wait_send()
    for u in range(2):
        x_copy(LAST, 2, u, 1).wait_send()
    y1_copy(LAST, 1).wait_send()
    y2_copy(LAST, 1).wait_send()
    z_copy(LAST, 1).wait_send()


def last_kernel(own1, far1, mats, gain, o_hbm, outv, o_sem):
    def o_copy(p):
        return pltpu.make_async_copy(outv.at[p], o_hbm.at[:, p], o_sem.at[p])

    for p in range(PASSES):
        current = dot(own1[p], mats[0]) + dot(far1[p], mats[1])
        power = jnp.sum(current * current, axis=-1, keepdims=True) / 256
        scaled = current * lax.rsqrt(power + EPSILON)
        outv[p, 0] = scaled[:, :256] * gain[...]
        outv[p, 1] = scaled[:, 256:] * gain[...]
        o_copy(p).start()
    for p in range(PASSES):
        o_copy(p).wait()


def shards(kernel_shard, sketch, projections, inverses, norm_gain):
    dma = pltpu.SemaphoreType.DMA
    vmem = pl.BlockSpec(memory_space=pltpu.VMEM)
    hbm = pl.BlockSpec(memory_space=pl.ANY)
    own1, far1, mats = pl.pallas_call(
        reduce_kernel,
        out_shape=(
            jax.ShapeDtypeStruct((3, 128, 256), BF16),
            jax.ShapeDtypeStruct((3, 128, 256), BF16),
            jax.ShapeDtypeStruct((2, 256, 512), BF16),
        ),
        in_specs=[hbm] * 4,
        out_specs=(vmem, vmem, vmem),
        scratch_shapes=[
            pltpu.VMEM((4, 2, 512, 2048), BF16),
            pltpu.VMEM((3, 2048, 256), BF16),
            pltpu.VMEM((3, 2048, 256), BF16),
            pltpu.VMEM((2, 2048, 256), BF16),
            pltpu.VMEM((2, 1, 2, 256, 128), BF16),
            pltpu.VMEM((2, 1, 2, 256, 256), BF16),
            pltpu.VMEM((2, 256, 256), BF16),
            pltpu.VMEM((2, 256, 256), BF16),
            pltpu.VMEM((3, 4, 256, 256), F32),
            pltpu.VMEM((3, 4, 256, 256), BF16),
            pltpu.VMEM((3, 4, 256, 256), BF16),
            pltpu.VMEM((3, 3, 2, 128, 256), BF16),
            pltpu.VMEM((3, 3, 2, 128, 256), BF16),
            pltpu.VMEM((3, 128, 256), BF16),
            pltpu.VMEM((3, 128, 256), BF16),
            pltpu.VMEM((3, 128, 256), BF16),
            pltpu.VMEM((3, 128, 256), F32),
            pltpu.VMEM((3, 128, 256), BF16),
            pltpu.VMEM((3, 128, 256), BF16),
            pltpu.VMEM((3, 128, 256), BF16),
            pltpu.VMEM((3, 128, 256), BF16),
            dma((4,)),
            dma((3,)),
            dma((2,)),
            dma((2,)),
            dma((2, 3, 4)),
            dma((2, 3, 4, 2)),
            dma((2, 4)),
            dma((2, 4)),
            dma((2, 4)),
        ],
        compiler_params=pltpu.CompilerParams(
            collective_id=0, has_side_effects=True, vmem_limit_bytes=56 << 20
        ),
        name="reduce_levels",
    )(kernel_shard, sketch, projections, inverses)
    return pl.pallas_call(
        last_kernel,
        out_shape=jax.ShapeDtypeStruct((2, 3, 128, 256), F32),
        in_specs=[vmem] * 4,
        out_specs=hbm,
        scratch_shapes=[pltpu.VMEM((3, 2, 128, 256), F32), dma((3,))],
        name="last_level",
    )(own1, far1, mats, norm_gain.reshape(1, 256))


def solution(mesh):
    torus = Mesh(mesh.devices.reshape(2, 4, 4, 2, 2), AXES)
    in_specs = (
        P(None, ("yl", "z"), ("x", "yh", "c")),
        P(None, ("x", "yh", "c"), None),
        P(None, ("yl", "z"), None, None, None),
        P(None, ("yl", "z"), None, None, None),
        P(),
    )
    return jax.shard_map(
        shards, mesh=torus, in_specs=in_specs, out_specs=P(None, None, AXES, None), check_vma=False
    )
```

time: 51.2 us -> 42.6 us (0.83)
  Pallas kernels: 48.9 us -> 42.5 us
  local copies, waits for them, and re-layouts: 2.1 us -> 0 us
    pallas_call x1 -> x2, Pallas kernels: 48.9 us -> 42.5 us  [the longest x1 40 us: shards(): pl.pallas_call(reduce_kernel, out_shape=(jax.ShapeDtypeStruct((3, 128, 25...]
    unnamed x1 -> x0, local copies, waits for them, and re-layouts: 2.1 us -> none
where the time goes in v2:
time: 42.6 us; the launch traced here: 42.5 us
  Pallas kernels  42.5 us (100%)
    pallas_call x1, Pallas kernels, shards(): pl.pallas_call(reduce_kernel, out_shape=(jax.ShapeDtypeStruct((3, 128, 25...  40 us
    pallas_call x1, Pallas kernels, shards(): pl.pallas_call(last_kernel, out_shape=jax.ShapeDtypeStruct((2, 3, 128, 25...  2.48 us

profile of v2, /device:TPU:0, one launch (start us, length us, event | category | flops | bytes accessed | tf_op | source)
XLA Modules:
  0.0 42.5 jit_solution(13002846987993988304)
XLA Ops:
  0.0 40.0 %reduce_levels.1 = (bf16[3,128,256]{2,1,0:T(8,128)(2,1)}, bf16[3,128,256]{2,1,0:T(8,128)(2,1)}, bf16[2,256,512]{2,1,0:T(8,128)(2,1)}) custom-call(bf16[2,2048,2048]{2,1,0:T(8,128)(2,1)} %k_hbm.1, bf16[3,2048,256]{2,1,0:T(8,128)(2,1)} %s_hbm.1, bf16[2,1,2,256,128]{4,3,2,1,0:T(8,128)(2,1)} %proj_hbm.1, bf16[2,1,2,256,256]{4,3,2,1,0:T(8,128)(2,1)} %inv_hbm.1), custom_call_target="tpu_custom_call" | custom-call | tf_op jit(solution)/shard_map/reduce_levels/pallas_call | solution.py:328
  40.0 2.5 %last_level.1 = f32[2,3,128,256]{3,2,1,0:T(8,128)} custom-call(bf16[3,128,256]{2,1,0:T(8,128)(2,1)} %get-tuple-element.8.own1, bf16[3,128,256]{2,1,0:T(8,128)(2,1)} %get-tuple-element.9.far1, bf16[2,256,512]{2,1,0:T(8,128)(2,1)} %get-tuple-element.10.mats, f32[1,256]{1,0:T(1,128)} %bitcast.1), custom_call_target="tpu_custom_call" | custom-call | tf_op jit(solution)/shard_map/last_level/pallas_call | solution.py:374

commit v3 on v2

--- a/solution.py
+++ b/solution.py
@@ -30,12 +30,15 @@
 
 
 def reduce_kernel(
-    k_hbm, s_hbm, proj_hbm, inv_hbm, own1_out, far1_out, mats_out,
-    kv, sv, pair, single, projv, invv, mats, mats_far,
-    own, c_send, c_recv, x_send, x_recv,
-    mine, y1_send, y1_recv, held, y2_send, y2_recv, own1, z_recv,
-    k_sem, s_sem, w_sem, m_sems, c_sems, x_sems, y1_sems, y2_sems, z_sems,
+    k_hbm, s_hbm, proj_hbm, inv_hbm, *refs,
 ):
+    outs = refs[:6]
+    (
+        kv, sv, pair, single, projv, invv, mats, mats_far, last_mats,
+        own, c_send, c_recv, x_send, x_recv,
+        mine, y1_send, y1_recv, held, y2_send, y2_recv, own1, z_recv, near_last,
+        k_sem, s_sem, w_sem, m_sems, c_sems, x_sems, y1_sems, y2_sems, z_sems,
+) = refs[6:]
     yl, z, x, yh, c = (lax.axis_index(a) for a in AXES)
     far_x = lax.rem(x + 2, 4)
     right = lax.rem(x + 1, 4)
@@ -55,22 +58,28 @@
     )
 
     def start_slab(j):
-        def start_part(part, _):
-            for core, core_idx in enumerate((1 - c, c)):
+        def start_half(half, _):
+            core = 1 - c + half * (2 * c - 1)
+            for part in range(2):
                 for u in range(2):
                     dest_x, dest_yh = units[j][u]
-                    row = pl.multiple_of(((dest_x * 2 + dest_yh) * 2 + core_idx) * 128, 128)
+                    row = pl.multiple_of(((dest_x * 2 + dest_yh) * 2 + core) * 128, 128)
+                    near = pl.multiple_of((half * 2 + u) * 128, 128)
                     pltpu.make_async_copy(
                         k_hbm.at[part, pl.ds(row, 128), :],
-                        kv.at[j, part, pl.ds((core * 2 + u) * 128, 128), :],
-                        k_sem.at[j],
+                        kv.at[j, part, pl.ds(near, 128), :],
+                        k_sem.at[j, half],
                     ).start()
             return 0
 
-        lax.fori_loop(0, 2, start_part, 0)
-
-    def wait_slab(j):
-        pltpu.make_async_copy(k_hbm.at[:, pl.ds(0, 512), :], kv.at[j], k_sem.at[j]).wait()
+        lax.fori_loop(0, 2, start_half, 0)
+
+    def wait_slab(j, half):
+        pltpu.make_async_copy(
+            k_hbm.at[:, pl.ds(0, 256), :],
+            kv.at[j, :, pl.ds(half * 256, 256), :],
+            k_sem.at[j, half],
+        ).wait()
 
     def s_copy(p):
         return pltpu.make_async_copy(s_hbm.at[p], sv.at[p], s_sem.at[p])
@@ -146,7 +155,7 @@
         rows = pl.ds(i * 128, 128)
         first = complex_block(invv[0, 0, 0, rows, :], invv[0, 0, 1, rows, :])
         mats[i] = dot(first, level).astype(BF16)
-        mats_out[i] = complex_block(invv[1, 0, 0, rows, :], invv[1, 0, 1, rows, :])
+        last_mats[i] = complex_block(invv[1, 0, 0, rows, :], invv[1, 0, 1, rows, :])
 
     def project_last():
         s_copy(LAST).wait()
@@ -213,37 +222,43 @@
         value = (held[p, rows, :] + y2_recv[p, rows, :].astype(F32)).astype(BF16)
         own1[p, rows, :] = value
         z_copy(p, h).start()
-        own1_out[p, rows, :] = value
+        near_last[p, rows, :] = dot(value, last_mats[0])
 
     def finish(p, h):
         z_copy(p, h).wait_recv()
         rows = span(p, h)
-        far1_out[p, rows, :] = z_recv[p, rows, :]
+        value = near_last[p, rows, :] + dot(z_recv[p, rows, :], last_mats[1])
+        outs[2 * p][rows, :] = value[:, :256]
+        outs[2 * p + 1][rows, :] = value[:, 256:]
 
     def pair_slab(j, _):
-        wait_slab(j)
+        wait_slab(j, 0)
+        wait_slab(j, 1)
         real_part = dot(kv[j, 0], pair[0])
         imag_part = dot(kv[j, 1], pair[1])
         cross = dot(kv[j, 0] + kv[j, 1], pair[2])
         real = real_part - imag_part
         imag = cross - real_part - imag_part
-
-        @pl.when(j == 0)
-        def _():
-            pl.semaphore_wait(barrier, 6)
-
         for p in range(2):
             cols = slice(p * 128, (p + 1) * 128)
             acc = jnp.concatenate([real[:, cols], imag[:, cols]], axis=1)
             c_send[p, j] = acc[:256].astype(BF16)
+            own[p, j] = acc[256:]
+
+        @pl.when(j == 0)
+        def _():
+            pl.semaphore_wait(barrier, 6)
+
+        for p in range(2):
             c_copy(p, j).start()
-            own[p, j] = acc[256:]
 
         @pl.when(j == 0)
         def _():
             m_copy().start()
-
-        for done in range(3):
+            post(0, 0)
+            post(1, 0)
+
+        for done in (1, 2):
 
             @pl.when(j == done + 1)
             def _():
@@ -262,21 +277,22 @@
         c_copy(LAST, j).start()
         own[LAST, j] = acc[256:]
 
-        @pl.when(j == 1)
-        def _():
-            post(LAST, 0)
-
-        @pl.when(j == 2)
-        def _():
-            post(LAST, 1)
-            finish_x(0, 0)
+        for done in range(3):
+
+            @pl.when(j == done + 1)
+            def _():
+                post(LAST, done)
+
+        for p in range(2):
+
+            @pl.when(j == p + 1)
+            def _():
+                finish_x(p, 0)
 
         return 0
 
     lax.fori_loop(0, 4, pair_slab, 0)
     lax.fori_loop(0, 4, single_slab, 0)
-    finish_x(1, 0)
-    post(LAST, 2)
     m_copy().wait()
     level_products(0, 0)
     level_products(1, 0)
@@ -286,9 +302,9 @@
     level_own(1, 0)
     level_products(LAST, 0)
     level_products(LAST, 1)
+    finish(0, 0)
     level_own(LAST, 0)
     level_own(LAST, 1)
-    finish(0, 0)
     finish(1, 0)
     finish(LAST, 0)
     finish(LAST, 1)
@@ -306,16 +322,18 @@
     z_copy(LAST, 1).wait_send()
 
 
-def last_kernel(own1, far1, mats, gain, o_hbm, outv, o_sem):
+def last_kernel(*refs):
+    gain, o_hbm, outv, o_sem = refs[6:]
+
     def o_copy(p):
         return pltpu.make_async_copy(outv.at[p], o_hbm.at[:, p], o_sem.at[p])
 
     for p in range(PASSES):
-        current = dot(own1[p], mats[0]) + dot(far1[p], mats[1])
-        power = jnp.sum(current * current, axis=-1, keepdims=True) / 256
-        scaled = current * lax.rsqrt(power + EPSILON)
-        outv[p, 0] = scaled[:, :256] * gain[...]
-        outv[p, 1] = scaled[:, 256:] * gain[...]
+        real, imag = refs[2 * p][...], refs[2 * p + 1][...]
+        power = jnp.sum(real * real + imag * imag, axis=-1, keepdims=True) / 256
+        scale = lax.rsqrt(power + EPSILON)
+        outv[p, 0] = real * scale * gain[...]
+        outv[p, 1] = imag * scale * gain[...]
         o_copy(p).start()
     for p in range(PASSES):
         o_copy(p).wait()
@@ -325,15 +343,11 @@
     dma = pltpu.SemaphoreType.DMA
     vmem = pl.BlockSpec(memory_space=pltpu.VMEM)
     hbm = pl.BlockSpec(memory_space=pl.ANY)
-    own1, far1, mats = pl.pallas_call(
+    current = pl.pallas_call(
         reduce_kernel,
-        out_shape=(
-            jax.ShapeDtypeStruct((3, 128, 256), BF16),
-            jax.ShapeDtypeStruct((3, 128, 256), BF16),
-            jax.ShapeDtypeStruct((2, 256, 512), BF16),
-        ),
+        out_shape=[jax.ShapeDtypeStruct((128, 256), F32)] * 6,
         in_specs=[hbm] * 4,
-        out_specs=(vmem, vmem, vmem),
+        out_specs=[vmem] * 6,
         scratch_shapes=[
             pltpu.VMEM((4, 2, 512, 2048), BF16),
             pltpu.VMEM((3, 2048, 256), BF16),
@@ -343,6 +357,7 @@
             pltpu.VMEM((2, 1, 2, 256, 256), BF16),
             pltpu.VMEM((2, 256, 256), BF16),
             pltpu.VMEM((2, 256, 256), BF16),
+            pltpu.VMEM((2, 256, 512), BF16),
             pltpu.VMEM((3, 4, 256, 256), F32),
             pltpu.VMEM((3, 4, 256, 256), BF16),
             pltpu.VMEM((3, 4, 256, 256), BF16),
@@ -356,7 +371,8 @@
             pltpu.VMEM((3, 128, 256), BF16),
             pltpu.VMEM((3, 128, 256), BF16),
             pltpu.VMEM((3, 128, 256), BF16),
-            dma((4,)),
+            pltpu.VMEM((3, 128, 512), F32),
+            dma((4, 2)),
             dma((3,)),
             dma((2,)),
             dma((2,)),
@@ -367,18 +383,19 @@
             dma((2, 4)),
         ],
         compiler_params=pltpu.CompilerParams(
-            collective_id=0, has_side_effects=True, vmem_limit_bytes=56 << 20
+            collective_id=0, has_side_effects=True, vmem_limit_bytes=54400 << 10
         ),
         name="reduce_levels",
     )(kernel_shard, sketch, projections, inverses)
     return pl.pallas_call(
         last_kernel,
         out_shape=jax.ShapeDtypeStruct((2, 3, 128, 256), F32),
-        in_specs=[vmem] * 4,
+        in_specs=[vmem] * 7,
         out_specs=hbm,
         scratch_shapes=[pltpu.VMEM((3, 2, 128, 256), F32), dma((3,))],
+        compiler_params=pltpu.CompilerParams(vmem_limit_bytes=8 << 20),
         name="last_level",
-    )(own1, far1, mats, norm_gain.reshape(1, 256))
+    )(*current, norm_gain.reshape(1, 256))
 
 
 def solution(mesh):

time: 42.6 us -> 40.5 us (0.951)
  Pallas kernels: 42.5 us -> 40.4 us
    pallas_call x1, Pallas kernels: 2.48 us -> 1.02 us  [shards(): pl.pallas_call(last_kernel, out_shape=jax.ShapeDtypeStruct((2, 3, 128, 25...]
    pallas_call x1, Pallas kernels: 40 us -> 39.3 us  [shards(): pl.pallas_call(reduce_kernel, out_shape=[jax.ShapeDtypeStruct((128, 256),...]
where the time goes in v3:
time: 40.5 us; the launch traced here: 40.4 us
  Pallas kernels  40.4 us (100%)
    pallas_call x1, Pallas kernels, shards(): pl.pallas_call(reduce_kernel, out_shape=[jax.ShapeDtypeStruct((128, 256),...  39.3 us
    pallas_call x1, Pallas kernels, shards(): pl.pallas_call(last_kernel, out_shape=jax.ShapeDtypeStruct((2, 3, 128, 25...  1.02 us

profile of v3, /device:TPU:0, one launch (start us, length us, event | category | flops | bytes accessed | tf_op | source)
XLA Modules:
  0.0 40.4 jit_solution(14895839211805848437)
XLA Ops:
  0.0 0.0 copy-start
  0.0 39.3 %reduce_levels.1 = (f32[128,256]{1,0:T(8,128)S(1)}, f32[128,256]{1,0:T(8,128)S(1)}, f32[128,256]{1,0:T(8,128)S(1)}, f32[128,256]{1,0:T(8,128)S(1)}, f32[128,256]{1,0:T(8,128)S(1)}, /*index=5*/f32[128,256]{1,0:T(8,128)S(1)}) custom-call(bf16[2,2048,2048]{2,1,0:T(8,128)(2,1)} %k_hbm.1, bf16[3,2048,256]{2,1,0:T(8,128)(2,1)} %s_hbm.1, ...), custom_call_target="tpu_custom_call" | custom-call | tf_op jit(solution)/shard_map/reduce_levels/pallas_call | solution.py:346
  39.4 0.0 copy-done
  39.4 1.0 %last_level.1 = f32[2,3,128,256]{3,2,1,0:T(8,128)} custom-call(f32[128,256]{1,0:T(8,128)S(1)} %get-tuple-element.11.refs_0_, f32[128,256]{1,0:T(8,128)S(1)} %get-tuple-element.12.refs_1_, f32[128,256]{1,0:T(8,128)S(1)} %get-tuple-element.13.refs_2_, f32[128,256]{1,0:T(8,128)S(1)} %get-tuple-element.14.refs_3_, f32[128,256]{1,0:T(8,128)S(1)} %get-tuple-element.15.refs_4_, ...), custom_call_target="tpu_custom_call" | custom-call | tf_op jit(solution)/shard_map/last_level/pallas_call | solution.py:390
Async XLA Ops:
  0.0 39.4 %copy-start = (f32[256]{0:T(256)S(1)}, f32[256]{0:T(256)}, u32[]{:S(2)}) copy-start(f32[256]{0:T(256)} %param.9) | copy-start | bytes 3076

commit v4 on v3

--- a/solution.py
+++ b/solution.py
@@ -124,8 +124,8 @@
     proj_copy.start()
     s_copy(0).start()
     s_copy(1).start()
+    inv_copy.start()
     start_slab(0)
-    inv_copy.start()
     start_slab(1)
     start_slab(2)
     start_slab(3)
@@ -295,12 +295,12 @@
     lax.fori_loop(0, 4, single_slab, 0)
     m_copy().wait()
     level_products(0, 0)
+    finish_x(LAST, 0)
     level_products(1, 0)
-    finish_x(LAST, 0)
     finish_x(LAST, 1)
     level_own(0, 0)
+    level_products(LAST, 0)
     level_own(1, 0)
-    level_products(LAST, 0)
     level_products(LAST, 1)
     finish(0, 0)
     level_own(LAST, 0)

time: 40.5 us -> 39.8 us (0.983)
  Pallas kernels: 40.4 us -> 39.6 us
    pallas_call x1, Pallas kernels: 39.3 us -> 38.6 us  [shards(): pl.pallas_call(reduce_kernel, out_shape=[jax.ShapeDtypeStruct((128, 256),...]
where the time goes in v4:
time: 39.8 us; the launch traced here: 39.7 us
  Pallas kernels  39.6 us (99%)
    pallas_call x1, Pallas kernels, shards(): pl.pallas_call(reduce_kernel, out_shape=[jax.ShapeDtypeStruct((128, 256),...  38.6 us
    pallas_call x1, Pallas kernels, shards(): pl.pallas_call(last_kernel, out_shape=jax.ShapeDtypeStruct((2, 3, 128, 25...  1.02 us

profile of v4, /device:TPU:0, one launch (start us, length us, event | category | flops | bytes accessed | tf_op | source)
XLA Modules:
  0.0 39.7 jit_solution(14840952921758389134)
XLA Ops:
  0.0 0.0 copy-start
  0.0 38.6 %reduce_levels.1 = (f32[128,256]{1,0:T(8,128)S(1)}, f32[128,256]{1,0:T(8,128)S(1)}, f32[128,256]{1,0:T(8,128)S(1)}, f32[128,256]{1,0:T(8,128)S(1)}, f32[128,256]{1,0:T(8,128)S(1)}, /*index=5*/f32[128,256]{1,0:T(8,128)S(1)}) custom-call(bf16[2,2048,2048]{2,1,0:T(8,128)(2,1)} %k_hbm.1, bf16[3,2048,256]{2,1,0:T(8,128)(2,1)} %s_hbm.1, ...), custom_call_target="tpu_custom_call" | custom-call | tf_op jit(solution)/shard_map/reduce_levels/pallas_call | solution.py:346
  38.6 0.0 copy-done
  38.6 1.0 %last_level.1 = f32[2,3,128,256]{3,2,1,0:T(8,128)} custom-call(f32[128,256]{1,0:T(8,128)S(1)} %get-tuple-element.11.refs_0_, f32[128,256]{1,0:T(8,128)S(1)} %get-tuple-element.12.refs_1_, f32[128,256]{1,0:T(8,128)S(1)} %get-tuple-element.13.refs_2_, f32[128,256]{1,0:T(8,128)S(1)} %get-tuple-element.14.refs_3_, f32[128,256]{1,0:T(8,128)S(1)} %get-tuple-element.15.refs_4_, ...), custom_call_target="tpu_custom_call" | custom-call | tf_op jit(solution)/shard_map/last_level/pallas_call | solution.py:390
Async XLA Ops:
  0.0 38.6 %copy-start = (f32[256]{0:T(256)S(1)}, f32[256]{0:T(256)}, u32[]{:S(2)}) copy-start(f32[256]{0:T(256)} %param.9) | copy-start | bytes 3076
